TPU v7x, 32 devices: a whole 2x2x4 slice. The times are simulated.
32 devices in a mesh: grp: 2 (over y), seq: 4 (over z), head: 2 (over x), sub: 2 (over core).
Axes of the slice: x: 2, y: 2, z: 4, core: 2. Of those that a mesh axis runs over, the one named last changes fastest.
Arguments:
- queries: float32 [1536, 2048], P(('grp', 'seq'), ('head', 'sub')), parts along dimension 0, may hold values from -6 to 6
- keys: float32 [1536, 2048], P(('grp', 'seq'), ('head', 'sub')), parts along dimension 0, may hold values from -6 to 6
- values: float32 [1536, 2048], P(('grp', 'seq'), ('head', 'sub')), parts along dimension 0, may hold values from -40 to 40
- opt_queries: float32 [16, 64, 2048], P(('grp', 'seq'), None, ('head', 'sub')), parts along dimension 0, may hold values from -6 to 6
- opt_keys: float32 [16, 64, 2048], P(('grp', 'seq'), None, ('head', 'sub')), parts along dimension 0, may hold values from -6 to 6
- opt_values: float32 [16, 64, 2048], P(('grp', 'seq'), None, ('head', 'sub')), parts along dimension 0, may hold values from -40 to 40
- opt_offsets: int32 [16], P(('grp', 'seq')), parts along dimension 0, may hold values from 0 to 192
- opt_lengths: int32 [16], P(('grp', 'seq')), parts along dimension 0, may hold values from 1 to 64, 320 in all
- norm_gain: float32 [2048], P(('head', 'sub')), may hold values from 0.5 to 2
- out_weight: bfloat16 [2048, 4096], P(('head', 'sub')), may hold values from -0.125 to 0.125
Outputs:
- ctx_out: bfloat16 [1536, 4096], P(('grp', 'seq'), ('head', 'sub')), parts along dimension 0
- opt_out: bfloat16 [16, 64, 4096], P(('grp', 'seq'), None, ('head', 'sub')), parts along dimension 0
There are 2 independent parts, one for each index of `grp`. A program takes and returns all parts, laid end to end along the dimension named above; an argument that names none is the same for every part. Nothing has to cross between parts.
Inputs may be any that keep to these rules, and one draw needn't show every extreme that they name: `opt_lengths`: within each scoring group the 8 lengths sum to 320, and the longest option of each group has exactly 64 tokens in every draw.
All inputs are finite; a program needn't handle non-finite values.
Results may differ from a plain program's by a relative error of at most 0.017.
Values may be sent and summed in bfloat16 or wider, within the bound.
A program may use at most 64 MiB of HBM per device.

v0:
```python
import jax
import jax.numpy as jnp
from jax import lax
from jax.sharding import PartitionSpec as P

DH = 128
norm_epsilon = 1e-05


def entering(value, axis, join, neutral):
    place = lax.axis_index(axis)
    gathered = lax.all_gather(value.astype(jnp.bfloat16), axis)
    state = jnp.zeros_like(value) + jnp.asarray(neutral, value.dtype)

    def one(hop, state):
        return join(state, lax.dynamic_index_in_dim(gathered, hop, 0, False).astype(value.dtype))

    return lax.fori_loop(0, place, one, state)


def head_norm(attended, gain, mask):
    mean_square = jnp.mean(attended * attended, axis=-1, keepdims=True)
    return (attended * lax.rsqrt(mean_square + norm_epsilon) * gain * mask).astype(jnp.bfloat16)


def combine_sum(earlier, later):
    return earlier + later


def grouped_project(rows, weight_columns, groups):
    count = rows.shape[0]
    flat = rows.reshape(count, groups, rows.shape[1] // groups)
    weight_groups = weight_columns.reshape(
        groups, weight_columns.shape[0] // groups, weight_columns.shape[1]
    )
    partial_value = jnp.einsum(
        "rgk,gkd->grd", flat, weight_groups, preferred_element_type=jnp.float32
    )
    partial_value = lax.optimization_barrier(partial_value.astype(jnp.bfloat16)).astype(jnp.float32)
    return jnp.sum(partial_value, axis=0).astype(jnp.bfloat16)


def on_device(
    queries,
    keys,
    values,
    opt_queries,
    opt_keys,
    opt_values,
    opt_offsets,
    opt_lengths,
    norm_gain,
    out_weight,
):
    highest = lax.Precision.HIGHEST
    tok_rows = queries.shape[0]
    heads = queries.shape[1] // DH
    opt_count = opt_queries.shape[0]
    slot_count = opt_queries.shape[1]
    group_count = lax.axis_size(("head", "sub"))
    weight_columns = lax.all_to_all(
        out_weight, ("head", "sub"), split_axis=1, concat_axis=0, tiled=True
    )
    block_q = queries.reshape(tok_rows, heads, DH)
    block_k = keys.reshape(tok_rows, heads, DH)
    block_v = values.reshape(tok_rows, heads, DH)
    gain = norm_gain.reshape(heads, DH)
    states = jnp.einsum("thd,the->hde", block_k, block_v, precision=highest)
    positions = jnp.arange(tok_rows, dtype=jnp.int32)
    causal = (positions[:, None] >= positions[None, :]).astype(jnp.float32)
    scores = jnp.einsum("thd,shd->hts", block_q, block_k, precision=highest) * causal[None]
    intra = jnp.einsum("hts,she->the", scores, block_v, precision=highest)
    opt_q = opt_queries.reshape(opt_count, slot_count, heads, DH)
    opt_k = opt_keys.reshape(opt_count, slot_count, heads, DH)
    opt_v = opt_values.reshape(opt_count, slot_count, heads, DH)
    before = (positions[None, :] < opt_offsets[:, None]).astype(jnp.float32)
    local = jnp.einsum("ot,thd,the->ohde", before, block_k, block_v, precision=highest)
    slots = jnp.arange(slot_count, dtype=jnp.int32)
    slot_causal = (slots[:, None] >= slots[None, :]).astype(jnp.float32)
    opt_scores = (
        jnp.einsum("oihd,ojhd->ohij", opt_q, opt_k, precision=highest) * slot_causal[None, None]
    )
    opt_intra = jnp.einsum("ohij,ojhe->oihe", opt_scores, opt_v, precision=highest)
    prefix = entering(states, "seq", combine_sum, jnp.zeros_like(states))
    inter = jnp.einsum("thd,hde->the", block_q, prefix, precision=highest)
    context_normed = head_norm(inter + intra, gain, 1.0).reshape(tok_rows, heads * DH)
    opt_state = prefix[None] + local
    opt_inter = jnp.einsum("oihd,ohde->oihe", opt_q, opt_state, precision=highest)
    valid = (slots[None, :] < opt_lengths[:, None]).astype(jnp.float32)
    opt_normed = head_norm(opt_inter + opt_intra, gain, valid[:, :, None, None]).reshape(
        opt_count * slot_count, heads * DH
    )
    gathered_ctx, gathered_opt = (
        lax.all_gather(context_normed, ("head", "sub"), axis=1, tiled=True),
        lax.all_gather(opt_normed, ("head", "sub"), axis=1, tiled=True),
    )
    context_out = grouped_project(gathered_ctx, weight_columns, group_count)
    opt_rows = grouped_project(gathered_opt, weight_columns, group_count)
    option_out = opt_rows.reshape(opt_count, slot_count, opt_rows.shape[1])
    return (context_out, option_out)


def solution(mesh):
    placed = (
        P(("grp", "seq"), ("head", "sub")),
        P(("grp", "seq"), ("head", "sub")),
        P(("grp", "seq"), ("head", "sub")),
        P(("grp", "seq"), None, ("head", "sub")),
        P(("grp", "seq"), None, ("head", "sub")),
        P(("grp", "seq"), None, ("head", "sub")),
        P(("grp", "seq")),
        P(("grp", "seq")),
        P(("head", "sub")),
        P(("head", "sub"), None),
    )
    return jax.shard_map(
        on_device,
        mesh=mesh,
        in_specs=placed,
        out_specs=(P(("grp", "seq"), ("head", "sub")), P(("grp", "seq"), None, ("head", "sub"))),
        check_vma=False,
    )
```

profile of v0, /device:TPU:0, one launch (start us, length us, event | category | flops | bytes accessed | tf_op | source)
XLA Modules:
  0.0 91.5 jit_solution(10964770409362976219)
XLA Ops:
  0.6 0.0 copy-start
  0.6 6.5 %copy.40 = bf16[512,4096]{0,1:T(8,128)(2,1)} copy(bf16[512,4096]{1,0:T(8,128)(2,1)} %param.21) | data formatting | bytes 8388608 | tf_op args[9]
  7.2 6.3 %copy.41 = bf16[512,4,1024]{2,0,1:T(8,128)(2,1)} copy(bf16[512,4,1024]{0,2,1:T(8,128)(2,1)} %bitcast.132) | data formatting | bytes 8388608 | tf_op jit(solution)/shard_map/all_to_all | solution.py:61
  13.5 0.0 copy-start.1
  13.5 5.0 %all-to-all-start = ((bf16[512,4,1024]{2,0,1:T(8,128)(2,1)}), bf16[512,4,1024]{2,0,1:T(8,128)(2,1)}, u32[]{:S(2)}, u32[]{:S(2)}) async-start(bf16[512,4,1024]{2,0,1:T(8,128)(2,1)} %copy.41), calls=%async_computation | async-start | bytes 8388608 | tf_op jit(solution)/shard_map/all_to_all | solution.py:61
  18.5 0.0 copy-start.8
  18.5 0.0 copy-start.4
  18.5 0.0 copy-start.5
  18.5 0.0 copy-start.9
  18.6 0.0 copy-done
  18.6 0.0 copy-done.1
  18.6 0.0 copy-start.6
  18.6 1.1 %convolution_convert_fusion = bf16[4,128,128]{2,1,0:T(8,128)(2,1)S(1)} fusion(f32[192,512]{1,0:T(8,128)S(1)} %copy-done.1, f32[192,512]{1,0:T(8,128)S(1)} %copy-done), kind=kOutput, calls=%fused_computation.17 | convolution fusion | flops 151060480 | bytes 917504 | tf_op jit(solution)/shard_map/thd,the->hde/dot_general | solution.py:68
  19.7 17.9 %all-gather = bf16[16,128,128]{2,1,0:T(8,128)(2,1)S(1)} all-gather(bf16[4,128,128]{2,1,0:T(8,128)(2,1)S(1)} %convolution_convert_fusion), channel_id=2, replica_groups=mesh['grp'=2,'seq'=4,'head'=2,'sub'=2] {'seq'}, dimensions={0}, use_global_device_ids=true | all-gather | bytes 655360 | tf_op jit(solution)/shard_map/all_gather | solution.py:12
  37.6 0.0 copy-start.7
  37.6 0.0 copy-done.8
  37.6 0.0 copy-start.3
  37.6 0.1 fusion.39
  37.7 0.0 copy-done.4
  37.7 0.0 copy-done.5
  37.7 0.5 convolution_multiply_fusion.1
  38.3 0.0 copy-done.9
  38.3 0.1 compare_convert_fusion.1
  38.4 1.9 %fusion.10 = f32[2,4,128,128]{3,2,1,0:T(8,128)S(1)} fusion(f32[192,4,128]{2,0,1:T(8,128)S(1)} %copy_bitcast_fusion, f32[192,2]{0,1:T(2,128)S(1)} %fusion.39, f32[4,128,128]{2,1,0:T(8,128)S(1)} %get-tuple-element.25, f32[192,512]{1,0:T(8,128)S(1)} %copy-done.1), kind=kOutput, calls=%fused_computation.9 | convolution fusion | flops 302317568 | bytes 1574400 | tf_op jit(solution)/shard_map/ot,thd,the->ohde/dot_general | solution.py:77
  40.3 0.6 convolution_bitcast_fusion.3
  40.9 0.0 copy-done.6
  40.9 0.5 multiply_reduce_fusion.1
  41.4 0.0 copy-done.7
  41.4 0.2 multiply_convert_fusion.1
  41.6 0.1 copy.49
  41.7 29.2 %all_gather.15 = bf16[128,2048]{1,0:T(8,128)(2,1)S(1)} all-gather(bf16[128,512]{1,0:T(8,128)(2,1)S(1)} %bitcast.136), channel_id=1, replica_groups=mesh['grp'=2,'seq'=4,'head'=2,'sub'=2] {'head','sub'}, dimensions={1}, use_global_device_ids=true | all-gather | bytes 655360 | tf_op jit(solution)/shard_map/all_gather | solution.py:95
  70.9 1.0 %copy.50 = bf16[128,2048]{0,1:T(8,128)(2,1)} copy(bf16[128,2048]{1,0:T(8,128)(2,1)S(1)} %all_gather.15) | data formatting | bytes 1048576 | tf_op jit(solution)/shard_map/all_gather | solution.py:95
  72.0 0.0 copy-done.3
  72.0 0.5 convolution_bitcast_fusion.1
  72.5 0.8 convolution_multiply_fusion
  73.3 1.0 %multiply_reduce_fusion = (f32[192,4]{0,1:T(4,128)S(1)}, f32[192,4,128]{2,0,1:T(8,128)S(1)}) fusion(f32[192,4,128]{2,0,1:T(8,128)S(1)} %convolution_bitcast_fusion.1, f32[4,192,192]{2,1,0:T(8,128)S(1)} %convolution_multiply_fusion, f32[192,512]{1,0:T(8,128)S(1)} %copy-done.1), kind=kOutput, calls=%fused_computation.31 | convolution fusion | flops 226786560 | bytes 1772544 | tf_op jit(solution)/shard_map/hts,she->the/dot_general | solution.py:72
  74.3 0.2 copy_bitcast_fusion.1
  74.5 8.7 %all_gather.14 = bf16[192,2048]{1,0:T(8,128)(2,1)S(1)} all-gather(bf16[192,512]{1,0:T(8,128)(2,1)S(1)} %copy_bitcast_fusion.1), channel_id=1, replica_groups=mesh['grp'=2,'seq'=4,'head'=2,'sub'=2] {'head','sub'}, dimensions={1}, use_global_device_ids=true | all-gather | bytes 983040 | tf_op jit(solution)/shard_map/all_gather | solution.py:94
  83.2 0.0 all-to-all-done
  83.2 0.0 copy-start.2
  83.2 3.2 %fusion.4 = bf16[4,192,1024]{2,1,0:T(8,128)(2,1)S(1)} fusion(bf16[512,4,1024]{2,0,1:T(8,128)(2,1)} %all-to-all-done, bf16[24,4,8,512]{3,2,1,0:T(8,128)(2,1)S(1)} %bitcast.133), kind=kOutput, calls=%fused_computation.5 | convolution fusion | flops 806092800 | bytes 6553600 | tf_op jit(solution)/shard_map/rgk,gkd->grd/dot_general | solution.py:36
  86.4 0.0 copy-done.2
  86.4 3.0 %fusion.7 = bf16[4,128,1024]{2,1,0:T(8,128)(2,1)S(1)} fusion(bf16[128,4,512]{0,2,1:T(8,128)(2,1)S(1)} %bitcast.134, bf16[512,4,1024]{2,0,1:T(8,128)(2,1)} %all-to-all-done), kind=kOutput, calls=%fused_computation.6 | convolution fusion | flops 537395200 | bytes 5767168 | tf_op jit(solution)/shard_map/rgk,gkd->grd/dot_general | solution.py:36
  89.4 1.1 %reduce_sum.43 = bf16[192,1024]{1,0:T(8,128)(2,1)} reduce(bf16[4,192,1024]{2,1,0:T(8,128)(2,1)S(1)} %fusion.4, bf16[]{:T(256)} %constant.28.clone.1), dimensions={0}, to_apply=%region_3.4 | reduce | flops 589824 | bytes 1966082 | tf_op jit(solution)/shard_map/reduce_sum | solution.py:40
  90.6 0.9 %reduce_sum.45 = bf16[128,1024]{1,0:T(8,128)(2,1)} reduce(bf16[4,128,1024]{2,1,0:T(8,128)(2,1)S(1)} %fusion.7, bf16[]{:T(256)} %constant.28.clone.1), dimensions={0}, to_apply=%region_5.6 | reduce | flops 393216 | bytes 1310722 | tf_op jit(solution)/shard_map/reduce_sum | solution.py:40
  (8 shorter events, 0.1 us)
Async XLA Ops:
  0.6 17.9 %copy-start = (f32[192,512]{1,0:T(8,128)S(1)}, f32[192,512]{1,0:T(8,128)}, u32[]{:S(2)}) copy-start(f32[192,512]{1,0:T(8,128)} %param.13) | copy-start | bytes 1179652
  13.5 5.1 %copy-start.1 = (f32[192,512]{1,0:T(8,128)S(1)}, f32[192,512]{1,0:T(8,128)}, u32[]{:S(2)}) copy-start(f32[192,512]{1,0:T(8,128)} %param.14) | copy-start | bytes 1179652
  13.5 69.7 %all-to-all-start = ((bf16[512,4,1024]{2,0,1:T(8,128)(2,1)}), bf16[512,4,1024]{2,0,1:T(8,128)(2,1)}, u32[]{:S(2)}, u32[]{:S(2)}) async-start(bf16[512,4,1024]{2,0,1:T(8,128)(2,1)} %copy.41), calls=%async_computation | async-start | bytes 8388608 | tf_op jit(solution)/shard_map/all_to_all | solution.py:61
  18.5 19.1 %copy-start.8 = (s32[2]{0:T(128)S(1)}, s32[2]{0:T(128)}, u32[]{:S(2)}) copy-start(s32[2]{0:T(128)} %param.18) | copy-start | bytes 28
  18.5 19.2 %copy-start.4 = (f32[2,64,512]{2,1,0:T(8,128)S(1)}, f32[2,64,512]{2,1,0:T(8,128)}, u32[]{:S(2)}) copy-start(f32[2,64,512]{2,1,0:T(8,128)} %param.15) | copy-start | bytes 786436
  18.5 19.2 %copy-start.5 = (f32[2,64,512]{2,1,0:T(8,128)S(1)}, f32[2,64,512]{2,1,0:T(8,128)}, u32[]{:S(2)}) copy-start(f32[2,64,512]{2,1,0:T(8,128)} %param.16) | copy-start | bytes 786436
  18.5 19.8 %copy-start.9 = (s32[2]{0:T(128)S(1)}, s32[2]{0:T(128)}, u32[]{:S(2)}) copy-start(s32[2]{0:T(128)} %param.19) | copy-start | bytes 28
  18.6 22.2 %copy-start.6 = (f32[2,64,512]{2,1,0:T(8,128)S(1)}, f32[2,64,512]{2,1,0:T(8,128)}, u32[]{:S(2)}) copy-start(f32[2,64,512]{2,1,0:T(8,128)} %param.17) | copy-start | bytes 786436
  37.6 3.8 %copy-start.7 = (f32[512]{0:T(512)S(1)}, f32[512]{0:T(512)}, u32[]{:S(2)}) copy-start(f32[512]{0:T(512)} %param.20) | copy-start | bytes 6148
  37.6 34.4 %copy-start.3 = (f32[192,512]{1,0:T(8,128)S(1)}, f32[192,512]{1,0:T(8,128)}, u32[]{:S(2)}) copy-start(f32[192,512]{1,0:T(8,128)} %param.12) | copy-start | bytes 1179652
  83.2 3.2 %copy-start.2 = (bf16[128,2048]{0,1:T(8,128)(2,1)S(1)}, bf16[128,2048]{0,1:T(8,128)(2,1)}, u32[]{:S(2)}) copy-start(bf16[128,2048]{0,1:T(8,128)(2,1)} %copy.50) | copy-start | bytes 1572868
where the time goes:
time: 92 us; the launch traced here: 91.5 us
  blocking collectives  55.8 us (61%)
  local copies, waits for them, and re-layouts  14.1 us (15%)
  matrix products  13.1 us (14%)
  starting transfers between devices  4.97 us (5%)
  other arithmetic  2.58 us (3%)
    all_gather x1, blocking collectives, on_device(): lax.all_gather(opt_normed, ('head', 'sub'), axis=1, tiled=True)  29.2 us
    all_gather x1, blocking collectives, entering(): gathered = lax.all_gather(value.astype(jnp.bfloat16), axis)  17.9 us
    all_gather x1, blocking collectives, on_device(): lax.all_gather(context_normed, ('head', 'sub'), axis=1, tiled=True)  8.71 us
    unnamed x22, local copies, waits for them, and re-layouts  6.62 us
    all_to_all x1, local copies, waits for them, and re-layouts, on_device(): lax.all_to_all(out_weight, ('head', 'sub'), split_axis=1, concat_axis=0,...  6.33 us
    dot_general x2, matrix products, grouped_project(): jnp.einsum('rgk,gkd->grd', flat, weight_groups, preferred_element_type=jn...  6.22 us
    all_to_all x1, starting transfers between devices, on_device(): lax.all_to_all(out_weight, ('head', 'sub'), split_axis=1, concat_axis=0,...  4.97 us
    reduce_sum x2, other arithmetic, grouped_project(): return jnp.sum(partial_value, axis=0).astype(jnp.bfloat16)  2.06 us
  transfers between devices with their start and end apart: 1, of which 0 were waited for; matrix products, arithmetic and copies ran while one was open for 9% of the time, Pallas kernels for 0%

commit v1 on v0

--- a/solution.py
+++ b/solution.py
@@ -91,7 +91,7 @@
         opt_count * slot_count, heads * DH
     )
     gathered_ctx, gathered_opt = (
-        lax.all_gather(context_normed, ("head", "sub"), axis=1, tiled=True),
+        jnp.concatenate(lax.all_gather(context_normed, ("head", "sub")), axis=1),
         lax.all_gather(opt_normed, ("head", "sub"), axis=1, tiled=True),
     )
     context_out = grouped_project(gathered_ctx, weight_columns, group_count)

time: 92 us -> 88.7 us (0.964)
  blocking collectives: 55.8 us -> 53.1 us
    all_gather x1, blocking collectives: 29.2 us -> 26.5 us  [on_device(): lax.all_gather(opt_normed, ('head', 'sub'), axis=1, tiled=True)]
    unnamed x22 -> x20, local copies, waits for them, and re-layouts: 6.62 us -> 6.66 us
where the time goes in v1:
time: 88.7 us; the launch traced here: 88.1 us
  blocking collectives  53.1 us (60%)
  local copies, waits for them, and re-layouts  13.6 us (15%)
  matrix products  13 us (15%)
  starting transfers between devices  4.98 us (6%)
  other arithmetic  2.57 us (3%)
  between operations  0.93 us (1%)
    all_gather x1, blocking collectives, on_device(): lax.all_gather(opt_normed, ('head', 'sub'), axis=1, tiled=True)  26.5 us
    all_gather x1, blocking collectives, entering(): gathered = lax.all_gather(value.astype(jnp.bfloat16), axis)  17.9 us
    all_gather x1, blocking collectives, on_device(): lax.all_gather(context_normed, ('head', 'sub'))  8.71 us
    unnamed x20, local copies, waits for them, and re-layouts  6.66 us
    all_to_all x1, local copies, waits for them, and re-layouts, on_device(): lax.all_to_all(out_weight, ('head', 'sub'), split_axis=1, concat_axis=0,...  6.29 us
    dot_general x2, matrix products, grouped_project(): jnp.einsum('rgk,gkd->grd', flat, weight_groups, preferred_element_type=jn...  6.14 us
    all_to_all x1, starting transfers between devices, on_device(): lax.all_to_all(out_weight, ('head', 'sub'), split_axis=1, concat_axis=0,...  4.98 us
    reduce_sum x2, other arithmetic, grouped_project(): return jnp.sum(partial_value, axis=0).astype(jnp.bfloat16)  2.06 us
  transfers between devices with their start and end apart: 1, of which 0 were waited for; matrix products, arithmetic and copies ran while one was open for 9% of the time, Pallas kernels for 0%

profile of v1, /device:TPU:0, one launch (start us, length us, event | category | flops | bytes accessed | tf_op | source)
XLA Modules:
  0.0 88.1 jit_solution(190686780942967769)
XLA Ops:
  0.6 0.0 copy-start
  0.6 6.6 %copy.39 = bf16[512,4096]{0,1:T(8,128)(2,1)} copy(bf16[512,4096]{1,0:T(8,128)(2,1)} %param.21) | data formatting | bytes 8388608 | tf_op args[9]
  7.2 6.3 %copy.40 = bf16[512,4,1024]{2,0,1:T(8,128)(2,1)} copy(bf16[512,4,1024]{0,2,1:T(8,128)(2,1)} %bitcast.126) | data formatting | bytes 8388608 | tf_op jit(solution)/shard_map/all_to_all | solution.py:61
  13.5 0.0 copy-start.1
  13.5 5.0 %all-to-all-start = ((bf16[512,4,1024]{2,0,1:T(8,128)(2,1)}), bf16[512,4,1024]{2,0,1:T(8,128)(2,1)}, u32[]{:S(2)}, u32[]{:S(2)}) async-start(bf16[512,4,1024]{2,0,1:T(8,128)(2,1)} %copy.40), calls=%async_computation | async-start | bytes 8388608 | tf_op jit(solution)/shard_map/all_to_all | solution.py:61
  18.5 0.0 copy-start.2
  18.5 0.0 copy-done
  18.6 0.0 copy-done.1
  18.6 1.1 %convolution_convert_fusion = bf16[4,128,128]{2,1,0:T(8,128)(2,1)S(1)} fusion(f32[192,512]{1,0:T(8,128)S(1)} %copy-done.1, f32[192,512]{1,0:T(8,128)S(1)} %copy-done), kind=kOutput, calls=%fused_computation.17 | convolution fusion | flops 151060480 | bytes 917504 | tf_op jit(solution)/shard_map/thd,the->hde/dot_general | solution.py:68
  19.6 17.9 %all-gather = bf16[16,128,128]{2,1,0:T(8,128)(2,1)S(1)} all-gather(bf16[4,128,128]{2,1,0:T(8,128)(2,1)S(1)} %convolution_convert_fusion), channel_id=2, replica_groups=mesh['grp'=2,'seq'=4,'head'=2,'sub'=2] {'seq'}, dimensions={0}, use_global_device_ids=true | all-gather | bytes 655360 | tf_op jit(solution)/shard_map/all_gather | solution.py:12
  37.6 0.0 copy-start.6
  37.6 0.0 copy-start.8
  37.6 0.0 copy-start.7
  37.6 0.0 copy-start.3
  37.6 0.0 copy-start.4
  37.6 0.0 copy-done.2
  37.6 0.5 convolution_bitcast_fusion.1
  38.1 0.8 convolution_multiply_fusion
  38.9 0.0 copy-start.5
  38.9 1.0 %multiply_reduce_fusion = (f32[192,4]{0,1:T(4,128)S(1)}, f32[192,4,128]{2,0,1:T(8,128)S(1)}) fusion(f32[192,4,128]{2,0,1:T(8,128)S(1)} %convolution_bitcast_fusion.1, f32[4,192,192]{2,1,0:T(8,128)S(1)} %convolution_multiply_fusion, f32[192,512]{1,0:T(8,128)S(1)} %copy-done.1), kind=kOutput, calls=%fused_computation.30 | convolution fusion | flops 226786560 | bytes 1772544 | tf_op jit(solution)/shard_map/hts,she->the/dot_general | solution.py:72
  39.9 0.0 copy-done.6
  39.9 0.2 multiply_convert_fusion
  40.1 0.2 copy.38
  40.3 0.1 all_gather_reshape.3
  40.4 0.0 copy-done.8
  40.4 0.1 compare_convert_fusion.1
  40.5 0.0 copy-done.7
  40.5 0.1 fusion.37
  40.6 0.0 copy-done.3
  40.6 0.0 copy-done.4
  40.6 0.5 convolution_multiply_fusion.1
  41.1 1.9 %fusion.10 = f32[2,4,128,128]{3,2,1,0:T(8,128)S(1)} fusion(f32[192,4,128]{2,0,1:T(8,128)S(1)} %copy_bitcast_fusion, f32[192,2]{0,1:T(2,128)S(1)} %fusion.37, f32[4,128,128]{2,1,0:T(8,128)S(1)} %get-tuple-element.25, f32[192,512]{1,0:T(8,128)S(1)} %copy-done.1), kind=kOutput, calls=%fused_computation.9 | convolution fusion | flops 302317568 | bytes 1574400 | tf_op jit(solution)/shard_map/ot,thd,the->ohde/dot_general | solution.py:77
  43.1 0.6 convolution_bitcast_fusion.3
  43.6 0.0 copy-done.5
  43.7 0.5 multiply_reduce_fusion.1
  44.2 0.2 multiply_convert_fusion.1
  44.3 0.1 copy.47
  44.5 26.5 %all_gather.15 = bf16[128,2048]{1,0:T(8,128)(2,1)S(1)} all-gather(bf16[128,512]{1,0:T(8,128)(2,1)S(1)} %bitcast.129), channel_id=1, replica_groups=mesh['grp'=2,'seq'=4,'head'=2,'sub'=2] {'head','sub'}, dimensions={1}, use_global_device_ids=true | all-gather | bytes 655360 | tf_op jit(solution)/shard_map/all_gather | solution.py:95
  70.9 0.3 copy.48
  71.2 8.7 %all_gather.14 = bf16[4,192,512]{2,1,0:T(8,128)(2,1)S(1)} all-gather(bf16[1,192,512]{2,1,0:T(8,128)(2,1)S(1)} %all_gather_reshape.3), channel_id=1, replica_groups=mesh['grp'=2,'seq'=4,'head'=2,'sub'=2] {'head','sub'}, dimensions={0}, use_global_device_ids=true | all-gather | bytes 983040 | tf_op jit(solution)/shard_map/all_gather | solution.py:94
  79.9 0.0 all-to-all-done
  79.9 3.2 %fusion.4 = bf16[4,192,1024]{2,1,0:T(8,128)(2,1)S(1)} fusion(bf16[512,4,1024]{2,0,1:T(8,128)(2,1)} %all-to-all-done, bf16[4,192,512]{2,1,0:T(8,128)(2,1)S(1)} %all_gather.14), kind=kOutput, calls=%fused_computation.5 | convolution fusion | flops 806092800 | bytes 6553600 | tf_op jit(solution)/shard_map/rgk,gkd->grd/dot_general | solution.py:36
  83.1 3.0 %fusion.7 = bf16[4,128,1024]{2,1,0:T(8,128)(2,1)S(1)} fusion(bf16[128,4,512]{0,2,1:T(8,128)(2,1)S(1)} %bitcast.127, bf16[512,4,1024]{2,0,1:T(8,128)(2,1)} %all-to-all-done), kind=kOutput, calls=%fused_computation.6 | convolution fusion | flops 537395200 | bytes 5767168 | tf_op jit(solution)/shard_map/rgk,gkd->grd/dot_general | solution.py:36
  86.1 1.1 %reduce_sum.43 = bf16[192,1024]{1,0:T(8,128)(2,1)} reduce(bf16[4,192,1024]{2,1,0:T(8,128)(2,1)S(1)} %fusion.4, bf16[]{:T(256)} %constant.28.clone.1), dimensions={0}, to_apply=%region_3.4 | reduce | flops 589824 | bytes 1966082 | tf_op jit(solution)/shard_map/reduce_sum | solution.py:40
  87.2 0.9 %reduce_sum.45 = bf16[128,1024]{1,0:T(8,128)(2,1)} reduce(bf16[4,128,1024]{2,1,0:T(8,128)(2,1)S(1)} %fusion.7, bf16[]{:T(256)} %constant.28.clone.1), dimensions={0}, to_apply=%region_5.6 | reduce | flops 393216 | bytes 1310722 | tf_op jit(solution)/shard_map/reduce_sum | solution.py:40
  (8 shorter events, 0.1 us)
Async XLA Ops:
  0.6 17.9 %copy-start = (f32[192,512]{1,0:T(8,128)S(1)}, f32[192,512]{1,0:T(8,128)}, u32[]{:S(2)}) copy-start(f32[192,512]{1,0:T(8,128)} %param.13) | copy-start | bytes 1179652
  13.5 5.0 %copy-start.1 = (f32[192,512]{1,0:T(8,128)S(1)}, f32[192,512]{1,0:T(8,128)}, u32[]{:S(2)}) copy-start(f32[192,512]{1,0:T(8,128)} %param.14) | copy-start | bytes 1179652
  13.5 66.4 %all-to-all-start = ((bf16[512,4,1024]{2,0,1:T(8,128)(2,1)}), bf16[512,4,1024]{2,0,1:T(8,128)(2,1)}, u32[]{:S(2)}, u32[]{:S(2)}) async-start(bf16[512,4,1024]{2,0,1:T(8,128)(2,1)} %copy.40), calls=%async_computation | async-start | bytes 8388608 | tf_op jit(solution)/shard_map/all_to_all | solution.py:61
  18.5 19.1 %copy-start.2 = (f32[192,512]{1,0:T(8,128)S(1)}, f32[192,512]{1,0:T(8,128)}, u32[]{:S(2)}) copy-start(f32[192,512]{1,0:T(8,128)} %param.12) | copy-start | bytes 1179652
  37.6 2.4 %copy-start.6 = (f32[512]{0:T(512)S(1)}, f32[512]{0:T(512)}, u32[]{:S(2)}) copy-start(f32[512]{0:T(512)} %param.20) | copy-start | bytes 6148
  37.6 2.8 %copy-start.8 = (s32[2]{0:T(128)S(1)}, s32[2]{0:T(128)}, u32[]{:S(2)}) copy-start(s32[2]{0:T(128)} %param.19) | copy-start | bytes 28
  37.6 2.9 %copy-start.7 = (s32[2]{0:T(128)S(1)}, s32[2]{0:T(128)}, u32[]{:S(2)}) copy-start(s32[2]{0:T(128)} %param.18) | copy-start | bytes 28
  37.6 3.0 %copy-start.3 = (f32[2,64,512]{2,1,0:T(8,128)S(1)}, f32[2,64,512]{2,1,0:T(8,128)}, u32[]{:S(2)}) copy-start(f32[2,64,512]{2,1,0:T(8,128)} %param.15) | copy-start | bytes 786436
  37.6 3.0 %copy-start.4 = (f32[2,64,512]{2,1,0:T(8,128)S(1)}, f32[2,64,512]{2,1,0:T(8,128)}, u32[]{:S(2)}) copy-start(f32[2,64,512]{2,1,0:T(8,128)} %param.16) | copy-start | bytes 786436
  38.9 4.7 %copy-start.5 = (f32[2,64,512]{2,1,0:T(8,128)S(1)}, f32[2,64,512]{2,1,0:T(8,128)}, u32[]{:S(2)}) copy-start(f32[2,64,512]{2,1,0:T(8,128)} %param.17) | copy-start | bytes 786436
